TPU v7x, 256 devices: a whole 4x4x8 slice. The times are simulated.
256 devices in a mesh: dp: 16 (over y_hi, x, core), ctx: 16 (over z, y_lo).
Axes of the slice: x: 4, y: 4 (y_hi: 2, y_lo: 2; y = y_hi * 2 + y_lo), z: 8, core: 2. Of those that a mesh axis runs over, the one named last changes fastest.
Arguments:
- queries: bfloat16 [65536, 2048], P(('dp', 'ctx')), parts along dimension 0, may hold values from -6 to 6
- key_states: bfloat16 [65536, 512], P(('dp', 'ctx')), parts along dimension 0, may hold values from -6 to 6
- value_states: bfloat16 [65536, 512], P(('dp', 'ctx')), parts along dimension 0, may hold values from -6 to 6
- grad_output: bfloat16 [65536, 2048], P(('dp', 'ctx')), parts along dimension 0, may hold values from -30 to 30
- log_norms: float32 [16, 65536], P(None, ('dp', 'ctx')), parts along dimension 1, may hold values from 6 to 7.5
- grad_dots: float32 [16, 65536], P(None, ('dp', 'ctx')), parts along dimension 1, may hold values from -150 to 150
- block_routes: int32 [256, 4], P(('dp', 'ctx')), parts along dimension 0, may hold values from 0 to 15, as said below
- owner_steps: int32 [64], P('dp'), parts along dimension 0, may hold values from 0 to 15, as said below
Outputs:
- grad_queries: bfloat16 [65536, 2048], P(('dp', 'ctx')), parts along dimension 0
- grad_keys: bfloat16 [65536, 512], P(('dp', 'ctx')), parts along dimension 0
- grad_values: bfloat16 [65536, 512], P(('dp', 'ctx')), parts along dimension 0
There are 16 independent parts, one for each index of `dp`. A program takes and returns all parts, laid end to end along the dimension named above; each array names one. Nothing has to cross between parts.
Inputs may be any that keep to these rules, and one draw needn't show every extreme that they name: block_routes[b, 0] = b; every entry of row b lies between 0 and b; entries of a row may repeat. `owner_steps`: 4 distinct indices of devices along ctx; device c along ctx holds block c.
All inputs are finite; a program needn't handle non-finite values.
Results may differ from a plain program's by a relative error of at most 0.0065.
Values may be sent and summed in bfloat16 or wider, within the bound.
A program may use at most 128 MiB of HBM per device.

v0:
```python
import math
import jax
import jax.numpy as jnp
from jax import lax
from jax.sharding import PartitionSpec as P

HQ = 16
HK = 4
DH = 128
BLK = 256


def broadcast(value, axis, source):
    kept = jnp.where(lax.axis_index(axis) == source, value, 0).astype(value.dtype)
    return lax.psum(kept, axis)


def pair_terms(query_rows, grad_rows, norm_rows, dot_rows, key_rows, value_rows, allowed):
    rows = query_rows.shape[0]
    cols = key_rows.shape[0]
    group = HQ // HK
    scale = 1.0 / math.sqrt(DH)
    query_heads = query_rows.reshape(rows, HK, group, DH)
    grad_heads = grad_rows.reshape(rows, HK, group, DH)
    key_heads = key_rows.reshape(cols, HK, DH)
    value_heads = value_rows.reshape(cols, HK, DH)
    scores = (
        jnp.einsum("qhgd,khd->hgqk", query_heads, key_heads, preferred_element_type=jnp.float32)
        * scale
    )
    norms = norm_rows.reshape(HK, group, rows, 1)
    dots = dot_rows.reshape(HK, group, rows, 1)
    probs = jnp.where(allowed, jnp.exp(scores - norms), jnp.float32(0.0))
    grad_probs = jnp.einsum(
        "qhgd,khd->hgqk", grad_heads, value_heads, preferred_element_type=jnp.float32
    )
    grad_scores = (probs * (grad_probs - dots)).astype(jnp.bfloat16)
    probs_low = probs.astype(jnp.bfloat16)
    grad_q = (
        jnp.einsum(
            "hgqk,khd->qhgd", grad_scores, key_heads, preferred_element_type=jnp.float32
        ).reshape(rows, HQ * DH)
        * scale
    )
    grad_k = (
        jnp.einsum(
            "hgqk,qhgd->khd", grad_scores, query_heads, preferred_element_type=jnp.float32
        ).reshape(cols, HK * DH)
        * scale
    )
    grad_v = jnp.einsum(
        "hgqk,qhgd->khd", probs_low, grad_heads, preferred_element_type=jnp.float32
    ).reshape(cols, HK * DH)
    return (grad_q, grad_k, grad_v)


def allowed_rows(local_routes, query_start, key_start, tokens, widen, active):
    per_dev = local_routes.shape[0]
    query_blocks = query_start // BLK + jnp.arange(per_dev, dtype=jnp.int32)
    key_blocks = key_start // BLK + jnp.arange(per_dev, dtype=jnp.int32)
    listed = jnp.any(local_routes[:, :, None] == key_blocks[None, None, :], axis=1)
    same = query_blocks[:, None] == key_blocks[None, :]
    chosen = listed & (same | widen) & active
    token_level = jnp.broadcast_to(chosen[:, None, :, None], (per_dev, BLK, per_dev, BLK)).reshape(
        tokens, tokens
    )
    positions = jnp.arange(tokens, dtype=jnp.int32)
    causal = key_start + positions[None, :] <= query_start + positions[:, None]
    return token_level & causal


def on_device(
    queries, key_states, value_states, grad_output, log_norms, grad_dots, block_routes, owner_steps
):
    tokens = queries.shape[0]
    device = lax.axis_index("ctx")
    start = device * tokens
    steps = owner_steps.shape[0]
    is_mine = owner_steps == device
    covered = jnp.any(is_mine)
    local_mask = allowed_rows(block_routes, start, start, tokens, covered, jnp.ones((), jnp.bool_))
    grad_q, grad_k, grad_v = pair_terms(
        queries, grad_output, log_norms, grad_dots, key_states, value_states, local_mask
    )
    for step in range(steps):
        owner = owner_steps[step]
        key_part, value_part = (
            broadcast(key_states, "ctx", owner),
            broadcast(value_states, "ctx", owner),
        )
        step_mask = allowed_rows(
            block_routes, start, owner * tokens, tokens, jnp.ones((), jnp.bool_), owner != device
        )
        term_q, term_k, term_v = pair_terms(
            queries, grad_output, log_norms, grad_dots, key_part, value_part, step_mask
        )
        grad_q = grad_q + term_q
        summed_k, summed_v = lax.psum((term_k, term_v), "ctx")
        taken = owner == device
        grad_k = grad_k + jnp.where(taken, summed_k, jnp.float32(0.0))
        grad_v = grad_v + jnp.where(taken, summed_v, jnp.float32(0.0))
    return (grad_q.astype(jnp.bfloat16), grad_k.astype(jnp.bfloat16), grad_v.astype(jnp.bfloat16))


def solution(mesh):
    return jax.shard_map(
        on_device,
        mesh=mesh,
        in_specs=(
            P(("dp", "ctx"), None),
            P(("dp", "ctx"), None),
            P(("dp", "ctx"), None),
            P(("dp", "ctx"), None),
            P(None, ("dp", "ctx")),
            P(None, ("dp", "ctx")),
            P(("dp", "ctx"), None),
            P("dp"),
        ),
        out_specs=(P(("dp", "ctx"), None), P(("dp", "ctx"), None), P(("dp", "ctx"), None)),
        check_vma=False,
    )
```

profile of v0, /device:TPU:1, one launch (start us, length us, event | category | flops | bytes accessed | tf_op | source)
XLA Modules:
  0.0 443.0 jit_solution(8952580223633291503)
XLA Ops:
  31.8 134.1 %all-reduce.7.cloned.1.call-done = (bf16[256,4,128]{2,0,1:T(8,128)(2,1)}, bf16[256,4,128]{2,0,1:T(8,128)(2,1)}, bf16[256,4,128]{2,0,1:T(8,128)(2,1)}, bf16[256,4...) async-done(((bf16[256,4,128]{2,0,1:T(8,128)(2,1)}, ...) | async-done | bytes 2097168 | tf_op jit(solution)/shard_map/psum | solution.py:15
  167.5 1.9 copy-done.6
  171.5 3.9 fusion.1
  177.0 2.0 copy.116
  180.2 1.8 fusion.27
  182.0 2.7 fusion.5
  184.7 2.1 copy.128
  186.8 3.2 fusion.59
  190.0 2.1 copy.113
  193.3 1.8 fusion.29
  195.0 2.7 fusion.9
  197.7 2.1 copy.125
  199.8 3.2 fusion.58
  203.0 2.0 copy.110
  206.3 1.8 fusion.31
  208.1 2.9 fusion.13
  210.9 2.0 copy.121
  213.0 3.2 fusion.57
  216.2 2.0 copy.106
  228.8 2.1 copy.107
  230.9 3.5 fusion.33
  241.8 190.2 %all-reduce.5.cloned.1.call-done = (f32[256,512]{1,0:T(8,128)}, f32[256,512]{1,0:T(8,128)}, f32[256,512]{1,0:T(8,128)}, f32[256,512]{1,0:T(8,128)}, f32[256,512]...) async-done(((f32[256,512]{1,0:T(8,128)}, f32[256,512]{1,0:T(8,128)}, f32[256,512]{1,0:T(8,128)}, f32[256,512]{1,0:T(8,128)}, ...) | async-done | bytes 4194320 | tf_op jit(solution)/shard_map/psum | solution.py:98
  432.1 2.1 add_convert_fusion.1
  434.1 2.1 add_convert_fusion
  (120 shorter events, 38.4 us)
Async XLA Ops:
  7.2 158.7 %all-reduce.7.cloned.1.call-start = ((), (), s32[]{:S(2)}) async-start(), calls=%async_computation.1 | async-start | bytes 4194304 | tf_op jit(solution)/shard_map/psum | solution.py:15
  13.4 12.2 %copy-start.27 = (f32[16,256]{1,0:T(8,128)S(1)}, f32[16,256]{1,0:T(8,128)}, u32[]{:S(2)}) copy-start(f32[16,256]{1,0:T(8,128)} %param.12) | copy-start | bytes 49156
  13.4 12.2 %copy-start.28 = (f32[16,256]{1,0:T(8,128)S(1)}, f32[16,256]{1,0:T(8,128)}, u32[]{:S(2)}) copy-start(f32[16,256]{1,0:T(8,128)} %param.13) | copy-start | bytes 49156
  13.6 12.1 %copy-start.9 = (bf16[256,2048]{1,0:T(8,128)(2,1)S(1)}, bf16[256,2048]{1,0:T(8,128)(2,1)}, u32[]{:S(2)}) copy-start(bf16[256,2048]{1,0:T(8,128)(2,1)} %param.8) | copy-start | bytes 3145732
  17.0 9.2 %copy-start.10 = (bf16[256,2048]{1,0:T(8,128)(2,1)S(1)}, bf16[256,2048]{1,0:T(8,128)(2,1)}, u32[]{:S(2)}) copy-start(bf16[256,2048]{1,0:T(8,128)(2,1)} %param.11) | copy-start | bytes 3145732
  17.0 9.8 %copy-start.34 = (s32[1,4]{1,0:T(1,128)S(1)}, s32[1,4]{1,0:T(1,128)}, u32[]{:S(2)}) copy-start(s32[1,4]{1,0:T(1,128)} %param.14) | copy-start | bytes 52
  20.4 411.7 %all-reduce.5.cloned.1.call-start = ((), (), s32[]{:S(2)}) async-start(), calls=%async_computation | async-start | bytes 8388608 | tf_op jit(solution)/shard_map/psum | solution.py:98
  25.7 145.8 %copy-start.29 = (f32[4,4,256]{2,1,0:T(4,128)}, f32[4,4,256]{2,1,0:T(4,128)S(1)}, u32[]{:S(2)}) copy-start(f32[4,4,256]{2,1,0:T(4,128)S(1)} %sub.89) | copy-start | bytes 49156
  26.8 143.7 %copy-start.11 = (bf16[256,2048]{0,1:T(8,128)(2,1)}, bf16[256,2048]{0,1:T(8,128)(2,1)S(1)}, u32[]{:S(2)}) copy-start(bf16[256,2048]{0,1:T(8,128)(2,1)S(1)} %copy.188) | copy-start | bytes 3145732
  175.4 3.6 copy-start.21
  179.7 2.3 copy-start.30
  179.7 2.3 copy-start.37
  184.7 7.3 %copy-start.19 = (bf16[256,4,128]{2,0,1:T(8,128)(2,1)S(1)}, bf16[256,4,128]{2,0,1:T(8,128)(2,1)}, u32[]{:S(2)}) copy-start(bf16[256,4,128]{2,0,1:T(8,128)(2,1)} %get-tuple-element.26) | copy-start | bytes 786436
  192.7 2.3 copy-start.31
  192.7 2.3 copy-start.36
  197.7 7.3 %copy-start.17 = (bf16[256,4,128]{2,0,1:T(8,128)(2,1)S(1)}, bf16[256,4,128]{2,0,1:T(8,128)(2,1)}, u32[]{:S(2)}) copy-start(bf16[256,4,128]{2,0,1:T(8,128)(2,1)} %get-tuple-element.28) | copy-start | bytes 786436
  205.8 2.3 copy-start.32
  205.8 2.3 copy-start.35
  213.0 7.9 %copy-start.16 = (bf16[256,512]{1,0:T(8,128)(2,1)S(1)}, bf16[256,512]{1,0:T(8,128)(2,1)}, u32[]{:S(2)}) copy-start(bf16[256,512]{1,0:T(8,128)(2,1)} %param.9) | copy-start | bytes 786436
  218.3 7.0 %copy-start.33 = (f32[4,4,256]{2,1,0:T(4,128)S(1)}, f32[4,4,256]{2,1,0:T(4,128)}, u32[]{:S(2)}) copy-start(f32[4,4,256]{2,1,0:T(4,128)} %copy-done.29) | copy-start | bytes 49156
  230.9 4.5 %copy-start.23 = (bf16[256,4,128]{2,0,1:T(8,128)(2,1)S(1)}, bf16[256,4,128]{2,0,1:T(8,128)(2,1)}, u32[]{:S(2)}) copy-start(bf16[256,4,128]{2,0,1:T(8,128)(2,1)} %get-tuple-element.22) | copy-start | bytes 786436
  235.4 2.3 copy-start.20
  239.4 192.7 %copy-start.8 = (f32[256,512]{1,0:T(8,128)S(1)}, f32[256,512]{1,0:T(8,128)}, u32[]{:S(2)}) copy-start(f32[256,512]{1,0:T(8,128)} %copy.107) | copy-start | bytes 1572868
  240.4 193.7 %copy-start.7 = (f32[256,512]{1,0:T(8,128)S(1)}, f32[256,512]{1,0:T(8,128)}, u32[]{:S(2)}) copy-start(f32[256,512]{1,0:T(8,128)} %copy.122) | copy-start | bytes 1572868
  (16 other events, 24.9 us)
Sparse Core Ops, SparseCore 0:
  20.5 145.3 all-reduce.6
  218.4 213.6 all-reduce.4
where the time goes:
time: 444 us; the launch traced here: 443 us
  waiting for transfers between devices  324 us (73%)
  matrix products  43.5 us (10%)
  local copies, waits for them, and re-layouts  41.1 us (9%)
  between operations  27.4 us (6%)
  other arithmetic  6.69 us (2%)
    psum x1, waiting for transfers between devices, on_device(): summed_k, summed_v = lax.psum((term_k, term_v), 'ctx')  190 us
    psum x1, waiting for transfers between devices, broadcast(): return lax.psum(kept, axis)  134 us
    dot_general x5, matrix products, pair_terms(): jnp.einsum('qhgd,khd->hgqk', grad_heads, value_heads, preferred_element_t...  13.5 us
    dot_general x5, matrix products, pair_terms(): jnp.einsum('hgqk,qhgd->khd', grad_scores, query_heads, preferred_element_...  12.8 us
    mul x5, local copies, waits for them, and re-layouts, pair_terms(): jnp.einsum('hgqk,qhgd->khd', grad_scores, query_heads, preferred_element_...  10.2 us
    unnamed x79, local copies, waits for them, and re-layouts  9.81 us
    dot_general x5, matrix products, pair_terms(): jnp.einsum('hgqk,qhgd->khd', probs_low, grad_heads, preferred_element_typ...  9.73 us
  transfers between devices with their start and end apart: 2, of which 2 were waited for; matrix products, arithmetic and copies ran while one was open for 5% of the time, Pallas kernels for 0%

commit v1 on v0

--- a/solution.py
+++ b/solution.py
@@ -12,7 +12,7 @@
 
 def broadcast(value, axis, source):
     kept = jnp.where(lax.axis_index(axis) == source, value, 0).astype(value.dtype)
-    return lax.psum(kept, axis)
+    return jnp.sum(lax.all_gather(kept, axis), axis=0)
 
 
 def pair_terms(query_rows, grad_rows, norm_rows, dot_rows, key_rows, value_rows, allowed):

time: 444 us -> 1100 us (2.48)
  waiting for transfers between devices: 324 us -> 952 us
  other arithmetic: 6.69 us -> 33.1 us
    all_gather x0 -> x8, waiting for transfers between devices: none -> 765 us  [broadcast(): return jnp.sum(lax.all_gather(kept, axis), axis=0)]
    psum x1 -> x0, waiting for transfers between devices: 134 us -> none  [broadcast(): return lax.psum(kept, axis)]
    reduce_sum x0 -> x8, other arithmetic: none -> 22.8 us  [broadcast(): return jnp.sum(lax.all_gather(kept, axis), axis=0)]
  transfers between devices with their start and end apart: 2 -> 9, of which waited for: 2 -> 9; matrix products, arithmetic and copies ran while one was open for 5% -> 5% of each run, Pallas kernels for 0% -> 0%
where the time goes in v1:
time: 1100 us
  waiting for transfers between devices  952 us (87%)
  matrix products  46.3 us (4%)
  local copies, waits for them, and re-layouts  40.1 us (4%)
  other arithmetic  33.1 us (3%)
  between operations  27.5 us (2%)
    all_gather x8, waiting for transfers between devices, broadcast(): return jnp.sum(lax.all_gather(kept, axis), axis=0)  765 us
    psum x1, waiting for transfers between devices, on_device(): summed_k, summed_v = lax.psum((term_k, term_v), 'ctx')  183 us
    reduce_sum x8, other arithmetic, broadcast(): return jnp.sum(lax.all_gather(kept, axis), axis=0)  22.8 us
  transfers between devices with their start and end apart: 9, of which 9 were waited for; matrix products, arithmetic and copies ran while one was open for 5% of the time, Pallas kernels for 0%

profile of v1, /device:TPU:1, one launch (start us, length us, event | category | flops | bytes accessed | tf_op | source)
XLA Modules:
  0.0 1099.4 jit_solution(407494161503366625)
XLA Ops:
  32.3 83.2 %all-gather.19.cloned.1.call-done = bf16[4096,512]{1,0:T(8,128)(2,1)} async-done(((bf16[256,512]{1,0:T(8,128)(2,1)}), bf16[4096,512]{1,0:T(8,128)(2,1)}) %all-gather.19.cloned.1.call-update) | async-done | bytes 4194320 | tf_op jit(solution)/shard_map/all_gather | solution.py:15
  115.5 2.8 reduce_sum.97
  119.2 97.3 %all-gather.23.cloned.1.call-done = bf16[4096,512]{1,0:T(8,128)(2,1)} async-done(((bf16[256,512]{1,0:T(8,128)(2,1)}), bf16[4096,512]{1,0:T(8,128)(2,1)}) %all-gather.23.cloned.1.call-update) | async-done | bytes 4194320 | tf_op jit(solution)/shard_map/all_gather | solution.py:15
  216.5 2.8 reduce_sum.99
  220.2 97.3 %all-gather.31.cloned.1.call-done = bf16[4096,512]{1,0:T(8,128)(2,1)} async-done(((bf16[256,512]{1,0:T(8,128)(2,1)}), bf16[4096,512]{1,0:T(8,128)(2,1)}) %all-gather.31.cloned.1.call-update) | async-done | bytes 4194320 | tf_op jit(solution)/shard_map/all_gather | solution.py:15
  317.5 2.8 reduce_sum.103
  321.2 97.2 %all-gather.27.cloned.1.call-done = bf16[4096,512]{1,0:T(8,128)(2,1)} async-done(((bf16[256,512]{1,0:T(8,128)(2,1)}), bf16[4096,512]{1,0:T(8,128)(2,1)}) %all-gather.27.cloned.1.call-update) | async-done | bytes 4194320 | tf_op jit(solution)/shard_map/all_gather | solution.py:15
  418.3 2.8 reduce_sum.101
  422.0 97.7 %all-gather.17.cloned.1.call-done = bf16[4096,512]{1,0:T(8,128)(2,1)} async-done(((bf16[256,512]{1,0:T(8,128)(2,1)}), bf16[4096,512]{1,0:T(8,128)(2,1)}) %all-gather.17.cloned.1.call-update) | async-done | bytes 4194320 | tf_op jit(solution)/shard_map/all_gather | solution.py:15
  519.8 2.8 reduce_sum.96
  522.9 98.3 %all-gather.21.cloned.1.call-done = bf16[4096,512]{1,0:T(8,128)(2,1)} async-done(((bf16[256,512]{1,0:T(8,128)(2,1)}), bf16[4096,512]{1,0:T(8,128)(2,1)}) %all-gather.21.cloned.1.call-update) | async-done | bytes 4194320 | tf_op jit(solution)/shard_map/all_gather | solution.py:15
  621.2 2.8 reduce_sum.98
  625.0 97.2 %all-gather.29.cloned.1.call-done = bf16[4096,512]{1,0:T(8,128)(2,1)} async-done(((bf16[256,512]{1,0:T(8,128)(2,1)}), bf16[4096,512]{1,0:T(8,128)(2,1)}) %all-gather.29.cloned.1.call-update) | async-done | bytes 4194320 | tf_op jit(solution)/shard_map/all_gather | solution.py:15
  722.2 2.8 reduce_sum.102
  726.0 97.2 %all-gather.25.cloned.1.call-done = bf16[4096,512]{1,0:T(8,128)(2,1)} async-done(((bf16[256,512]{1,0:T(8,128)(2,1)}), bf16[4096,512]{1,0:T(8,128)(2,1)}) %all-gather.25.cloned.1.call-update) | async-done | bytes 4194320 | tf_op jit(solution)/shard_map/all_gather | solution.py:15
  823.2 2.8 reduce_sum.100
  831.1 4.0 fusion.5
  847.2 3.2 fusion.60
  856.1 2.9 fusion.9
  861.0 3.2 fusion.58
  869.2 2.8 fusion.13
  874.1 3.2 fusion.57
  894.7 3.7 fusion.33
  905.9 182.8 %all-reduce.3.cloned.1.call-done = (f32[256,512]{1,0:T(8,128)}, f32[256,512]{1,0:T(8,128)}, f32[256,512]{1,0:T(8,128)}, f32[256,512]{1,0:T(8,128)}, f32[256,512]...) async-done(((f32[256,512]{1,0:T(8,128)}, f32[256,512]{1,0:T(8,128)}, f32[256,512]{1,0:T(8,128)}, f32[256,512]{1,0:T(8,128)}, ...) | async-done | bytes 4194320 | tf_op jit(solution)/shard_map/psum | solution.py:98
  (146 shorter events, 78.0 us)
Async XLA Ops:
  7.2 17.8 %copy-start.28 = (f32[16,256]{1,0:T(8,128)S(1)}, f32[16,256]{1,0:T(8,128)}, u32[]{:S(2)}) copy-start(f32[16,256]{1,0:T(8,128)} %param.12) | copy-start | bytes 49156
  7.2 17.8 %copy-start.29 = (f32[16,256]{1,0:T(8,128)S(1)}, f32[16,256]{1,0:T(8,128)}, u32[]{:S(2)}) copy-start(f32[16,256]{1,0:T(8,128)} %param.13) | copy-start | bytes 49156
  7.2 18.4 %copy-start.14 = (bf16[256,2048]{1,0:T(8,128)(2,1)S(1)}, bf16[256,2048]{1,0:T(8,128)(2,1)}, u32[]{:S(2)}) copy-start(bf16[256,2048]{1,0:T(8,128)(2,1)} %param.8) | copy-start | bytes 3145732
  7.2 18.9 %copy-start.15 = (bf16[256,2048]{1,0:T(8,128)(2,1)S(1)}, bf16[256,2048]{1,0:T(8,128)(2,1)}, u32[]{:S(2)}) copy-start(bf16[256,2048]{1,0:T(8,128)(2,1)} %param.11) | copy-start | bytes 3145732
  7.2 108.3 %all-gather.19.cloned.1.call-start = ((), (), s32[]{:S(2)}) async-start(), calls=%async_computation.1 | async-start | bytes 4456448 | tf_op jit(solution)/shard_map/all_gather | solution.py:15
  13.4 14.1 %copy-start.34 = (s32[1,4]{1,0:T(1,128)S(1)}, s32[1,4]{1,0:T(1,128)}, u32[]{:S(2)}) copy-start(s32[1,4]{1,0:T(1,128)} %param.14) | copy-start | bytes 52
  13.4 203.1 %all-gather.23.cloned.1.call-start = ((), (), s32[]{:S(2)}) async-start(), calls=%async_computation.3 | async-start | bytes 4456448 | tf_op jit(solution)/shard_map/all_gather | solution.py:15
  14.2 303.3 %all-gather.31.cloned.1.call-start = ((), (), s32[]{:S(2)}) async-start(), calls=%async_computation.7 | async-start | bytes 4456448 | tf_op jit(solution)/shard_map/all_gather | solution.py:15
  14.9 403.4 %all-gather.27.cloned.1.call-start = ((), (), s32[]{:S(2)}) async-start(), calls=%async_computation.5 | async-start | bytes 4456448 | tf_op jit(solution)/shard_map/all_gather | solution.py:15
  15.5 504.3 %all-gather.17.cloned.1.call-start = ((), (), s32[]{:S(2)}) async-start(), calls=%async_computation | async-start | bytes 4456448 | tf_op jit(solution)/shard_map/all_gather | solution.py:15
  17.5 603.7 %all-gather.21.cloned.1.call-start = ((), (), s32[]{:S(2)}) async-start(), calls=%async_computation.2 | async-start | bytes 4456448 | tf_op jit(solution)/shard_map/all_gather | solution.py:15
  18.0 704.2 %all-gather.29.cloned.1.call-start = ((), (), s32[]{:S(2)}) async-start(), calls=%async_computation.6 | async-start | bytes 4456448 | tf_op jit(solution)/shard_map/all_gather | solution.py:15
  18.8 804.4 %all-gather.25.cloned.1.call-start = ((), (), s32[]{:S(2)}) async-start(), calls=%async_computation.4 | async-start | bytes 4456448 | tf_op jit(solution)/shard_map/all_gather | solution.py:15
  19.5 1069.2 %all-reduce.3.cloned.1.call-start = ((), (), s32[]{:S(2)}) async-start(), calls=%async_computation.8 | async-start | bytes 8388608 | tf_op jit(solution)/shard_map/psum | solution.py:98
  32.3 794.8 %copy-start.27 = (pred[256,256]{0,1:T(8,128)(4,1)}, pred[256,256]{0,1:T(8,128)(4,1)S(1)}, u32[]{:S(2)}) copy-start(pred[256,256]{0,1:T(8,128)(4,1)S(1)} %get-tuple-element.35) | copy-start | bytes 196612
  826.1 3.0 copy-start.16
  826.3 3.7 copy-start.9
  866.9 2.3 copy-start.21
  866.9 2.3 copy-start.32
  879.3 9.7 copy-start.33
  894.7 4.7 copy-start.10
  899.5 2.3 copy-start.7
  903.4 185.3 %copy-start.13 = (f32[256,512]{1,0:T(8,128)S(1)}, f32[256,512]{1,0:T(8,128)}, u32[]{:S(2)}) copy-start(f32[256,512]{1,0:T(8,128)} %copy.160) | copy-start | bytes 1572868
  904.5 186.3 %copy-start.12 = (f32[256,512]{1,0:T(8,128)S(1)}, f32[256,512]{1,0:T(8,128)}, u32[]{:S(2)}) copy-start(f32[256,512]{1,0:T(8,128)} %copy.175) | copy-start | bytes 1572868
  (20 other events, 35.5 us)
Sparse Core Ops, SparseCore 0:
  13.5 101.8 all-gather.18
  117.3 99.1 all-gather.22
  218.3 99.1 all-gather.30
  319.1 99.1 all-gather.26
  420.5 99.1 all-gather.16
  522.0 99.1 all-gather.20
  623.0 99.1 all-gather.28
  724.0 99.1 all-gather.24
  879.5 209.1 all-reduce.2
